TPU v7x, 32 devices: a whole 2x2x4 slice. The times are simulated.
32 devices in a mesh: dp: 8 (over z, y), tensor: 4 (over x, core).
Axes of the slice: x: 2, y: 2, z: 4, core: 2. Of those that a mesh axis runs over, the one named last changes fastest.
Arguments:
- tokens: bfloat16 [6144, 1120], P('dp', 'tensor'), may hold values from -6 to 6
- first_gain: float32 [1120], replicated, may hold values from 0.5 to 1.5
- first_shift: float32 [1120], replicated, may hold values from -3 to 3
- triple_weight: bfloat16 [1120, 3, 1120], P(None, None, 'tensor'), may hold values from -0.1875 to 0.1875
- triple_bias: float32 [2, 1120], P(None, 'tensor'), may hold values from -3 to 3
- output_weight: bfloat16 [1120, 1120], P('tensor'), may hold values from -0.5 to 0.5
- output_bias: float32 [1120], replicated, may hold values from -3 to 3
- second_gain: float32 [1120], replicated, may hold values from 0.5 to 1.5
- second_shift: float32 [1120], replicated, may hold values from -3 to 3
- up_weight: bfloat16 [1120, 4480], P(None, 'tensor'), may hold values from -0.1875 to 0.1875
- up_bias: float32 [4480], P('tensor'), may hold values from -3 to 3
- down_weight: bfloat16 [4480, 1120], P('tensor'), may hold values from -0.09375 to 0.09375
- down_bias: float32 [1120], replicated, may hold values from -3 to 3
- cotangent: bfloat16 [6144, 1120], P('dp', 'tensor'), may hold values from -6 to 6
- lengths: int32 [16], P('dp'), may hold values from 96 to 384
Outputs:
- layer_out: bfloat16 [6144, 1120], P('dp', 'tensor')
- input_grad: bfloat16 [6144, 1120], P('dp', 'tensor')
- first_gain_grad: float32 [1120], replicated
- first_shift_grad: float32 [1120], replicated
- triple_weight_grad: float32 [1120, 3, 1120], P(None, None, 'tensor')
- triple_bias_grad: float32 [2, 1120], P(None, 'tensor')
- output_weight_grad: float32 [1120, 1120], P('tensor')
- output_bias_grad: float32 [1120], replicated
- second_gain_grad: float32 [1120], replicated
- second_shift_grad: float32 [1120], replicated
- up_weight_grad: float32 [1120, 4480], P(None, 'tensor')
- up_bias_grad: float32 [4480], P('tensor')
- down_weight_grad: float32 [4480, 1120], P('tensor')
- down_bias_grad: float32 [1120], replicated
All inputs are finite; a program needn't handle non-finite values.
Results may differ from a plain program's by a relative error of at most 0.019.
Values may be sent and summed in bfloat16 or wider, within the bound.
No kernel may reach another device: no remote copies, remote signals or barrier semaphores. Data moves between devices by JAX's collectives and lax.ppermute only.
A program may use at most 128 MiB of HBM per device.

v0:
```python
import jax
import jax.numpy as jnp
from jax import lax
from jax.sharding import PartitionSpec as P

HEAD_DIM = 56
CELL_LEN = 384
epsilon = 1e-05


def layer_norm(field, gain, shift):
    center = field - jnp.mean(field, -1, keepdims=True)
    spread = jnp.mean(center * center, -1, keepdims=True)
    return center * lax.rsqrt(spread + epsilon) * gain + shift


def smooth_gate(field):
    return jax.nn.gelu(field, approximate=True)


def body(
    tokens,
    first_gain,
    first_shift,
    triple_weight,
    triple_bias,
    output_weight,
    output_bias,
    second_gain,
    second_shift,
    up_weight,
    up_bias,
    down_weight,
    down_bias,
    cotangent,
    lengths,
):
    row_count = tokens.shape[0]
    share_width = tokens.shape[1]
    width = triple_weight.shape[0]
    head_width = triple_weight.shape[2]
    local_heads = head_width // HEAD_DIM
    cell_count = row_count // CELL_LEN
    factor = HEAD_DIM ** (-0.5)
    offset = lax.axis_index("tensor") * share_width
    shape = (cell_count, CELL_LEN, local_heads, HEAD_DIM)
    whole_rows = lax.all_gather(tokens, "tensor", axis=1, tiled=True)
    floats = whole_rows.astype(jnp.float32)
    first_normed = layer_norm(floats, first_gain, first_shift).astype(jnp.bfloat16)
    triple_flat = triple_weight.reshape(width, 3 * head_width)
    projected = jnp.dot(first_normed, triple_flat, preferred_element_type=jnp.float32)
    projected = projected.reshape(row_count, 3, head_width)
    queries = (projected[:, 0] + triple_bias[0]).astype(jnp.bfloat16).reshape(shape)
    key_rows = projected[:, 1].astype(jnp.bfloat16).reshape(shape)
    value_rows = (projected[:, 2] + triple_bias[1]).astype(jnp.bfloat16).reshape(shape)
    places = jnp.arange(CELL_LEN)
    allowed = (places[None, None, :] <= places[None, :, None]) & (
        places[None, None, :] < lengths[:, None, None]
    )
    allowed = allowed[:, None]
    scores = (
        jnp.einsum("cqhd,ckhd->chqk", queries, key_rows, preferred_element_type=jnp.float32)
        * factor
    )
    masked = jnp.where(allowed, scores, -1e30)
    largest = jnp.max(masked, -1, keepdims=True)
    expo = jnp.exp(masked - largest)
    probs = expo / jnp.sum(expo, -1, keepdims=True)
    probs_low = probs.astype(jnp.bfloat16)
    context = jnp.einsum(
        "chqk,ckhd->cqhd", probs_low, value_rows, preferred_element_type=jnp.float32
    )
    context = context.reshape(row_count, head_width).astype(jnp.bfloat16)
    partial_value = jnp.dot(context, output_weight, preferred_element_type=jnp.float32)
    resid_full = (
        floats
        + lax.psum(partial_value.astype(jnp.bfloat16), "tensor").astype(jnp.float32)
        + output_bias
    )
    resid_share = lax.dynamic_slice_in_dim(resid_full, offset, share_width, 1)
    second_normed = layer_norm(resid_full, second_gain, second_shift).astype(jnp.bfloat16)
    hidden_pre = jnp.dot(second_normed, up_weight, preferred_element_type=jnp.float32) + up_bias
    hidden = smooth_gate(hidden_pre).astype(jnp.bfloat16)
    down_part = jnp.dot(hidden, down_weight, preferred_element_type=jnp.float32)
    down_total = lax.psum_scatter(
        down_part.astype(jnp.bfloat16), "tensor", scatter_dimension=1, tiled=True
    ).astype(jnp.float32)
    layer_out = (
        resid_share + down_total + lax.dynamic_slice_in_dim(down_bias, offset, share_width)
    ).astype(jnp.bfloat16)
    grad_rows = lax.all_gather(cotangent, "tensor", axis=1, tiled=True)
    grad_float = grad_rows.astype(jnp.float32)
    down_bias_grad = jnp.sum(grad_float, 0)
    down_grad = jnp.einsum("rf,rd->fd", hidden, grad_rows, preferred_element_type=jnp.float32)
    hidden_grad = jnp.einsum(
        "rd,fd->rf", grad_rows, down_weight, preferred_element_type=jnp.float32
    )
    gate_value, gate_back = jax.vjp(smooth_gate, hidden_pre)
    pre_grad = gate_back(hidden_grad)[0]
    up_bias_grad = jnp.sum(pre_grad, 0)
    pre_low = pre_grad.astype(jnp.bfloat16)
    up_grad = jnp.einsum("rd,rf->df", second_normed, pre_low, preferred_element_type=jnp.float32)
    normed_part = jnp.einsum("rf,df->rd", pre_low, up_weight, preferred_element_type=jnp.float32)
    normed_grad = lax.psum(normed_part.astype(jnp.bfloat16), "tensor").astype(jnp.float32)
    norm_value, second_back = jax.vjp(layer_norm, resid_full, second_gain, second_shift)
    resid_back, second_gain_grad, second_shift_grad = second_back(normed_grad)
    resid_grad = grad_float + resid_back
    output_bias_grad = jnp.sum(resid_grad, 0)
    resid_low = resid_grad.astype(jnp.bfloat16)
    output_grad = jnp.einsum("rh,rd->hd", context, resid_low, preferred_element_type=jnp.float32)
    context_grad = jnp.einsum(
        "rd,hd->rh", resid_low, output_weight, preferred_element_type=jnp.float32
    )
    context_grad = context_grad.astype(jnp.bfloat16).reshape(shape)
    prob_grad = jnp.einsum(
        "cqhd,ckhd->chqk", context_grad, value_rows, preferred_element_type=jnp.float32
    )
    value_grad = jnp.einsum(
        "chqk,cqhd->ckhd", probs_low, context_grad, preferred_element_type=jnp.float32
    )
    score_grad = probs * (prob_grad - jnp.sum(prob_grad * probs, -1, keepdims=True))
    score_low = (score_grad * factor).astype(jnp.bfloat16)
    query_grad = jnp.einsum(
        "chqk,ckhd->cqhd", score_low, key_rows, preferred_element_type=jnp.float32
    )
    key_grad = jnp.einsum("chqk,cqhd->ckhd", score_low, queries, preferred_element_type=jnp.float32)
    query_grad = query_grad.reshape(row_count, head_width)
    key_grad = key_grad.reshape(row_count, head_width)
    value_grad = value_grad.reshape(row_count, head_width)
    triple_bias_grad = jnp.stack([jnp.sum(query_grad, 0), jnp.sum(value_grad, 0)], 0)
    triple_low = jnp.stack([query_grad, key_grad, value_grad], 1).astype(jnp.bfloat16)
    triple_low = triple_low.reshape(row_count, 3 * head_width)
    triple_grad = jnp.einsum(
        "rd,rc->dc", first_normed, triple_low, preferred_element_type=jnp.float32
    )
    triple_grad = triple_grad.reshape(width, 3, head_width)
    first_part = jnp.einsum(
        "rc,dc->rd", triple_low, triple_flat, preferred_element_type=jnp.float32
    )
    first_grad = lax.psum(first_part.astype(jnp.bfloat16), "tensor").astype(jnp.float32)
    first_value, first_back = jax.vjp(layer_norm, floats, first_gain, first_shift)
    input_back, first_gain_grad, first_shift_grad = first_back(first_grad)
    input_full = resid_grad + input_back
    input_grad = lax.dynamic_slice_in_dim(input_full, offset, share_width, 1).astype(jnp.bfloat16)
    summed = lax.psum(
        (
            first_gain_grad,
            first_shift_grad,
            triple_grad,
            triple_bias_grad,
            output_grad,
            output_bias_grad,
            down_grad,
            down_bias_grad,
            up_grad,
            up_bias_grad,
            second_gain_grad,
            second_shift_grad,
        ),
        "dp",
    )
    return (
        layer_out,
        input_grad,
        summed[0],
        summed[1],
        summed[2],
        summed[3],
        summed[4],
        summed[5],
        summed[10],
        summed[11],
        summed[8],
        summed[9],
        summed[6],
        summed[7],
    )


def solution(mesh):
    placed = (
        P("dp", "tensor"),
        P(),
        P(),
        P(None, None, "tensor"),
        P(None, "tensor"),
        P("tensor", None),
        P(),
        P(),
        P(),
        P(None, "tensor"),
        P("tensor"),
        P("tensor", None),
        P(),
        P("dp", "tensor"),
        P("dp"),
    )
    return jax.shard_map(
        body,
        mesh=mesh,
        in_specs=placed,
        out_specs=(
            P("dp", "tensor"),
            P("dp", "tensor"),
            P(),
            P(),
            P(None, None, "tensor"),
            P(None, "tensor"),
            P("tensor", None),
            P(),
            P(),
            P(),
            P(None, "tensor"),
            P("tensor"),
            P("tensor", None),
            P(),
        ),
        check_vma=False,
    )
```

profile of v0, /device:TPU:0, one launch (start us, length us, event | category | flops | bytes accessed | tf_op | source)
XLA Modules:
  0.0 791.9 jit_solution(13180206961236640351)
XLA Ops:
  11.4 21.4 %all-gather.3.cloned.1.call-done = bf16[768,1120]{0,1:T(8,128)(2,1)} async-done(((bf16[768,280]{0,1:T(8,128)(2,1)}), bf16[768,1120]{0,1:T(8,128)(2,1)}) %all-gather.3.cloned.1.call-update) | async-done | bytes 1720336 | tf_op jit(solution)/shard_map/all_gather | solution.py:47
  36.7 3.7 fusion.40
  46.0 2.5 squeeze.8
  48.6 6.1 fusion.107
  54.7 3.4 fusion.61
  59.3 2.3 convolution_convert_fusion.2
  61.9 6.4 fusion.120
  68.3 39.0 %all-reduce.7.cloned.1.call-done = bf16[768,1120]{0,1:T(8,128)(2,1)} async-done(((bf16[768,1120]{0,1:T(8,128)(2,1)}), bf16[768,1120]{0,1:T(8,128)(2,1)}) %all-reduce.7.cloned.1.call-update) | async-done | bytes 1720336 | tf_op jit(solution)/shard_map/psum | solution.py:77
  107.2 2.6 fusion.104
  110.7 2.4 copy-done.25
  113.1 6.6 fusion.100
  120.9 3.6 convolution_convert_fusion
  125.0 45.1 %all-reduce.9.cloned.1.call-done = bf16[768,1120]{0,1:T(8,128)(2,1)} async-done(((bf16[768,1120]{0,1:T(8,128)(2,1)}), bf16[768,1120]{0,1:T(8,128)(2,1)}) %all-reduce.9.cloned.1.call-update) | async-done | bytes 1720336 | tf_op jit(solution)/shard_map/psum | solution.py:104
  170.1 3.6 convert_reduce_fusion.1
  173.8 3.8 fusion.32
  182.2 4.0 fusion.112
  186.3 3.7 fusion.79
  190.0 9.7 %fusion.53 = bf16[2,384,5,56]{1,3,2,0:T(8,128)(2,1)S(1)} fusion(f32[2,5,384,384]{2,3,1,0:T(8,128)} %fusion.79, f32[2,5,384,384]{2,3,1,0:T(8,128)} %get-tuple-element.47, f32[2,5,384]{2,1,0:T(8,128)S(1)} %copy-done.29, f32[2,384,5,56]{1,0,3,2:T(2,128)S(1)} %copy-done.15, f32[5,56]{1,0:T(8,128)S(1)} %add.148), kind=kOutput, calls=%fused_computation.72 | convolution fusion | flops 175906944 | bytes 13103200 | tf_op jit(solution)/shard_map/chqk,cqhd->ckhd/dot_general | solution.py:126
  199.7 9.8 %fusion.113 = (f32[5,56]{1,0:T(8,128)S(1)}, bf16[2,384,5,56]{1,3,2,0:T(8,128)(2,1)S(1)}) fusion(f32[2,5,384,384]{2,3,1,0:T(8,128)} %fusion.79, f32[2,5,384,384]{2,3,1,0:T(8,128)} %get-tuple-element.47, f32[2,5,384]{2,1,0:T(8,128)S(1)} %copy-done.29, bf16[2,384,5,56]{1,0,3,2:T(2,128)(2,1)S(1)} %copy-done.18), kind=kOutput, calls=%fused_computation.132 | convolution fusion | flops 175906656 | bytes 12673120 | tf_op jit(solution)/shard_map/chqk,ckhd->cqhd/dot_general | solution.py:123
  211.5 4.8 fusion.34
  216.4 6.8 convolution_convert_fusion.1
  223.3 7.5 fusion.99
  230.8 5.0 fusion.70
  237.7 3.9 fusion.56
  242.6 19.3 %all-reduce.11.cloned.1.call-done = bf16[768,1120]{0,1:T(8,128)(2,1)} async-done(((bf16[768,1120]{0,1:T(8,128)(2,1)}), bf16[768,1120]{0,1:T(8,128)(2,1)}) %all-reduce.11.cloned.1.call-update) | async-done | bytes 1720336 | tf_op jit(solution)/shard_map/psum | solution.py:140
  261.9 2.9 fusion.33
  264.8 38.2 %all-reduce = (f32[1120]{0:T(1024)}, f32[1120]{0:T(1024)}, f32[2,280]{1,0:T(2,128)}, f32[1120]{0:T(1024)}, f32[1120]{0:T(1024)}, /*index=5*/f32[1120]{0:T(1024)}, f32[1120]{0:T(1024)}, f32[1120]{0:T(1024)}) all-reduce(f32[1120]{0:T(1024)S(1)} %get-tuple-element.16, ...), channel_id=1, replica_groups=mesh['dp'=8,'tensor'=4] {'dp'}, use_global_device_ids=true, to_apply=%region_16.17 | all-reduce | flops 8400 | bytes 67200 | tf_op jit(solution)/shard_map/psum | solution.py:145
  303.0 2.5 fusion.103
  309.8 463.3 %all-reduce.13.cloned.1.call-done = (f32[1120,3,280]{0,2,1:T(8,128)}, f32[280,1120]{1,0:T(8,128)}, f32[1120,1120]{1,0:T(8,128)}, f32[1120,1120]{1,0:T(8,128)}) async-done(((f32[1120,3,280]{0,2,1:T(8,128)}, f32[280,1120]{1,0:T(8,128)}, f32[1120,1120]{1,0:T(8,128)}, f32[1120,1120]{1,0:T(8,128)}), (f32[1120,3,280]{0,2,1:T(8,128)}, f32[280,1120]{1,0:T(8,128)}, f32[1120,1120]{1,0:T(8,128)}, ...) | async-done | bytes 15052816 | tf_op jit(solution)/shard_map/psum | solution.py:145
  773.1 4.5 copy.99
  778.7 2.6 copy.101
  782.5 2.3 copy.102
  (125 shorter events, 33.6 us)
Async XLA Ops:
  7.2 103.1 %copy-start = (bf16[1120,1120]{1,0:T(8,128)(2,1)S(1)}, bf16[1120,1120]{1,0:T(8,128)(2,1)}, u32[]{:S(2)}) copy-start(bf16[1120,1120]{1,0:T(8,128)(2,1)} %param.24) | copy-start | bytes 7526404
  7.2 29.5 %copy-start.24 = (f32[1120]{0:T(1024)S(1)}, f32[1120]{0:T(1024)}, u32[]{:S(2)}) copy-start(f32[1120]{0:T(1024)} %param.17) | copy-start | bytes 13444
  7.2 29.5 %copy-start.20 = (f32[1120]{0:T(1024)S(1)}, f32[1120]{0:T(1024)}, u32[]{:S(2)}) copy-start(f32[1120]{0:T(1024)} %param.16) | copy-start | bytes 13444
  7.2 25.6 %all-gather.3.cloned.1.call-start = ((), (), s32[]{:S(2)}) async-start(), calls=%async_computation.1 | async-start | bytes 2150400 | tf_op jit(solution)/shard_map/all_gather | solution.py:47
  8.0 53.9 %all-gather.5.cloned.1.call-start = ((), (), s32[]{:S(2)}) async-start(), calls=%async_computation.4 | async-start | bytes 2150400 | tf_op jit(solution)/shard_map/all_gather | solution.py:91
  8.7 98.5 %all-reduce.7.cloned.1.call-start = ((), (), s32[]{:S(2)}) async-start(), calls=%async_computation.2 | async-start | bytes 3440640 | tf_op jit(solution)/shard_map/psum | solution.py:77
  32.8 3.9 copy-start.5
  54.7 3.4 copy-start.28
  54.7 4.6 copy-start.16
  61.6 45.6 %copy-start.21 = (f32[1120]{0:T(1024)S(1)}, f32[1120]{0:T(1024)}, u32[]{:S(2)}) copy-start(f32[1120]{0:T(1024)} %param.21) | copy-start | bytes 13444
  61.6 108.5 %all-reduce.9.cloned.1.call-start = ((), (), s32[]{:S(2)}) async-start(), calls=%async_computation.5 | async-start | bytes 3440640 | tf_op jit(solution)/shard_map/psum | solution.py:104
  109.8 9.9 %copy-start.2 = (f32[768,1120]{0,1:T(8,128)}, f32[768,1120]{0,1:T(8,128)S(1)}, u32[]{:S(2)}) copy-start(f32[768,1120]{0,1:T(8,128)S(1)} %get-tuple-element.42) | copy-start | bytes 10321924
  124.6 137.3 %all-reduce.11.cloned.1.call-start = ((), (), s32[]{:S(2)}) async-start(), calls=%async_computation.6 | async-start | bytes 3440640 | tf_op jit(solution)/shard_map/psum | solution.py:140
  170.1 3.7 copy-start.9
  173.8 3.9 copy-start.3
  173.8 3.9 copy-start.12
  177.7 3.7 copy-start.17
  186.3 3.7 copy-start.15
  190.0 9.7 %copy-start.18 = (bf16[2,384,5,56]{1,0,3,2:T(2,128)(2,1)S(1)}, bf16[2,384,5,56]{1,0,3,2:T(2,128)(2,1)}, u32[]{:S(2)}) copy-start(bf16[2,384,5,56]{1,0,3,2:T(2,128)(2,1)} %convert_element_type.93) | copy-start | bytes 1290244
  216.3 91.3 %reduce-scatter.2.cloned.1.call-start = ((), (), s32[]{:S(2)}) async-start(), calls=%async_computation.3 | async-start | bytes 2150400 | tf_op jit(solution)/shard_map/reduce_scatter | solution.py:85
  216.3 6.9 copy-start.13
  223.2 550.0 %all-reduce.13.cloned.1.call-start = ((), (), s32[]{:S(2)}) async-start(), calls=%async_computation.7 | async-start | bytes 30965760 | tf_op jit(solution)/shard_map/psum | solution.py:145
  223.2 7.5 copy-start.4
  223.3 7.5 copy-start.27
  230.8 5.1 copy-start.8
  230.8 5.1 copy-start.11
  773.1 5.5 slice-start.2
  773.1 4.5 copy-start.14
  773.1 5.5 slice-start.3
  777.6 4.3 slice-start
  778.7 3.9 slice-start.1
  778.7 6.2 copy-start.1
  (9 other events, 13.7 us)
Sparse Core Ops, SparseCore 0:
  9.6 23.1 all-gather.2
  34.4 20.4 all-gather.4
  61.7 45.4 all-reduce.6
  124.7 45.4 all-reduce.8
  216.4 45.4 all-reduce.10
  264.3 28.8 reduce-scatter.1
  299.1 473.9 all-reduce.12
where the time goes:
time: 799 us; the launch traced here: 792 us
  waiting for transfers between devices  590 us (74%)
  matrix products  89.9 us (11%)
  blocking collectives  38.2 us (5%)
  local copies, waits for them, and re-layouts  30.8 us (4%)
  other arithmetic  27.7 us (3%)
  between operations  14.8 us (2%)
    psum x1, waiting for transfers between devices, body(): lax.psum((first_gain_grad, first_shift_grad, triple_grad, triple_bias_gra...  463 us
    psum x1, waiting for transfers between devices, body(): lax.psum(normed_part.astype(jnp.bfloat16), 'tensor').astype(jnp.float32)  45.1 us
    psum x1, waiting for transfers between devices, body(): lax.psum(partial_value.astype(jnp.bfloat16), 'tensor').astype(jnp.float32)  39 us
    psum x1, blocking collectives, body(): lax.psum((first_gain_grad, first_shift_grad, triple_grad, triple_bias_gra...  38.2 us
    all_gather x1, waiting for transfers between devices, body(): whole_rows = lax.all_gather(tokens, 'tensor', axis=1, tiled=True)  21.4 us
    psum x1, waiting for transfers between devices, body(): lax.psum(first_part.astype(jnp.bfloat16), 'tensor').astype(jnp.float32)  19.3 us
    unnamed x73, local copies, waits for them, and re-layouts  18.4 us
  transfers between devices with their start and end apart: 7, of which 5 were waited for; matrix products, arithmetic and copies ran while one was open for 9% of the time, Pallas kernels for 0%

commit v1 on v0

--- a/solution.py
+++ b/solution.py
@@ -74,7 +74,9 @@
     partial_value = jnp.dot(context, output_weight, preferred_element_type=jnp.float32)
     resid_full = (
         floats
-        + lax.psum(partial_value.astype(jnp.bfloat16), "tensor").astype(jnp.float32)
+        + jnp.sum(lax.all_gather(partial_value.astype(jnp.bfloat16), "tensor"), axis=0).astype(
+            jnp.float32
+        )
         + output_bias
     )
     resid_share = lax.dynamic_slice_in_dim(resid_full, offset, share_width, 1)

time: 799 us -> 830 us (1.039)
  local copies, waits for them, and re-layouts: 30.8 us -> 44.5 us
  other arithmetic: 27.7 us -> 38.9 us
    all_gather x0 -> x1, waiting for transfers between devices: none -> 43.4 us  [body(): lax.all_gather(partial_value.astype(jnp.bfloat16), 'tensor')]
    psum x1 -> x0, waiting for transfers between devices: 39 us -> none  [body(): lax.psum(partial_value.astype(jnp.bfloat16), 'tensor').astype(jnp.float32)]
    all_gather x0 -> x1, local copies, waits for them, and re-layouts: none -> 13.7 us  [body(): lax.all_gather(partial_value.astype(jnp.bfloat16), 'tensor')]
    reduce_sum x0 -> x1, other arithmetic: none -> 11.2 us  [body(): jnp.sum(lax.all_gather(partial_value.astype(jnp.bfloat16), 'tensor'), axi...]
where the time goes in v1:
time: 830 us; the launch traced here: 821 us
  waiting for transfers between devices  594 us (72%)
  matrix products  89.9 us (11%)
  local copies, waits for them, and re-layouts  44.5 us (5%)
  other arithmetic  38.9 us (5%)
  blocking collectives  38.2 us (5%)
  between operations  14.8 us (2%)
    psum x1, waiting for transfers between devices, body(): lax.psum((first_gain_grad, first_shift_grad, triple_grad, triple_bias_gra...  463 us
    psum x1, waiting for transfers between devices, body(): lax.psum(normed_part.astype(jnp.bfloat16), 'tensor').astype(jnp.float32)  45.1 us
    all_gather x1, waiting for transfers between devices, body(): lax.all_gather(partial_value.astype(jnp.bfloat16), 'tensor')  43.4 us
    psum x1, blocking collectives, body(): lax.psum((first_gain_grad, first_shift_grad, triple_grad, triple_bias_gra...  38.2 us
    all_gather x1, waiting for transfers between devices, body(): whole_rows = lax.all_gather(tokens, 'tensor', axis=1, tiled=True)  21.4 us
    psum x1, waiting for transfers between devices, body(): lax.psum(first_part.astype(jnp.bfloat16), 'tensor').astype(jnp.float32)  19.3 us
    unnamed x73, local copies, waits for them, and re-layouts  18.4 us
  transfers between devices with their start and end apart: 7, of which 5 were waited for; matrix products, arithmetic and copies ran while one was open for 9% of the time, Pallas kernels for 0%

profile of v1, /device:TPU:0, one launch (start us, length us, event | category | flops | bytes accessed | tf_op | source)
XLA Modules:
  0.0 821.1 jit_solution(16990289322420340971)
XLA Ops:
  11.4 21.4 %all-gather.5.cloned.1.call-done = bf16[768,1120]{0,1:T(8,128)(2,1)} async-done(((bf16[768,280]{0,1:T(8,128)(2,1)}), bf16[768,1120]{0,1:T(8,128)(2,1)}) %all-gather.5.cloned.1.call-update) | async-done | bytes 1720336 | tf_op jit(solution)/shard_map/all_gather | solution.py:47
  36.7 3.7 fusion.40
  46.0 2.5 squeeze.8
  48.6 6.1 fusion.107
  54.6 3.4 fusion.61
  61.7 6.4 fusion.120
  68.0 43.4 %all-gather.9.cloned.1.call-done = bf16[3072,1120]{0,1:T(8,128)(2,1)} async-done(((bf16[768,1120]{0,1:T(8,128)(2,1)}), bf16[3072,1120]{0,1:T(8,128)(2,1)}) %all-gather.9.cloned.1.call-update) | async-done | bytes 6881296 | tf_op jit(solution)/shard_map/all_gather | solution.py:77
  111.5 13.7 %reshape.175 = bf16[4,768,1120]{1,0,2:T(4,128)(2,1)} reshape(bf16[3072,1120]{0,1:T(8,128)(2,1)} %all-gather.9.cloned.1.call-done) | data formatting | bytes 13762560 | tf_op jit(solution)/shard_map/all_gather | solution.py:77
  125.2 11.2 %reduce_sum.184 = bf16[768,1120]{0,1:T(8,128)(2,1)} reduce(bf16[4,768,1120]{1,0,2:T(4,128)(2,1)} %reshape.175, bf16[]{:T(256)} %constant.34.clone.1), dimensions={0}, to_apply=%region_4.5 | reduce | flops 2580480 | bytes 8601602 | tf_op jit(solution)/shard_map/reduce_sum | solution.py:77
  136.4 2.6 fusion.104
  139.8 2.4 copy-done.25
  142.3 6.6 fusion.100
  150.1 3.6 convolution_convert_fusion
  154.1 45.1 %all-reduce.6.cloned.1.call-done = bf16[768,1120]{0,1:T(8,128)(2,1)} async-done(((bf16[768,1120]{0,1:T(8,128)(2,1)}), bf16[768,1120]{0,1:T(8,128)(2,1)}) %all-reduce.6.cloned.1.call-update) | async-done | bytes 1720336 | tf_op jit(solution)/shard_map/psum | solution.py:106
  199.2 3.6 convert_reduce_fusion.1
  202.9 3.8 fusion.32
  211.4 4.0 fusion.112
  215.5 3.7 fusion.79
  219.1 9.7 %fusion.53 = bf16[2,384,5,56]{1,3,2,0:T(8,128)(2,1)S(1)} fusion(f32[2,5,384,384]{2,3,1,0:T(8,128)} %fusion.79, f32[2,5,384,384]{2,3,1,0:T(8,128)} %get-tuple-element.47, f32[2,5,384]{2,1,0:T(8,128)S(1)} %copy-done.29, f32[2,384,5,56]{1,0,3,2:T(2,128)S(1)} %copy-done.15, f32[5,56]{1,0:T(8,128)S(1)} %add.146), kind=kOutput, calls=%fused_computation.72 | convolution fusion | flops 175906944 | bytes 13103200 | tf_op jit(solution)/shard_map/chqk,cqhd->ckhd/dot_general | solution.py:128
  228.9 9.8 %fusion.113 = (f32[5,56]{1,0:T(8,128)S(1)}, bf16[2,384,5,56]{1,3,2,0:T(8,128)(2,1)S(1)}) fusion(f32[2,5,384,384]{2,3,1,0:T(8,128)} %fusion.79, f32[2,5,384,384]{2,3,1,0:T(8,128)} %get-tuple-element.47, f32[2,5,384]{2,1,0:T(8,128)S(1)} %copy-done.29, bf16[2,384,5,56]{1,0,3,2:T(2,128)(2,1)S(1)} %copy-done.18), kind=kOutput, calls=%fused_computation.132 | convolution fusion | flops 175906656 | bytes 12673120 | tf_op jit(solution)/shard_map/chqk,ckhd->cqhd/dot_general | solution.py:125
  240.7 4.8 fusion.34
  245.6 6.8 convolution_convert_fusion.1
  252.4 7.5 fusion.99
  260.0 5.0 fusion.70
  266.9 3.9 fusion.56
  271.8 19.3 %all-reduce.8.cloned.1.call-done = bf16[768,1120]{0,1:T(8,128)(2,1)} async-done(((bf16[768,1120]{0,1:T(8,128)(2,1)}), bf16[768,1120]{0,1:T(8,128)(2,1)}) %all-reduce.8.cloned.1.call-update) | async-done | bytes 1720336 | tf_op jit(solution)/shard_map/psum | solution.py:142
  291.1 2.9 fusion.33
  294.0 38.2 %all-reduce = (f32[1120]{0:T(1024)}, f32[1120]{0:T(1024)}, f32[2,280]{1,0:T(2,128)}, f32[1120]{0:T(1024)}, f32[1120]{0:T(1024)}, /*index=5*/f32[1120]{0:T(1024)}, f32[1120]{0:T(1024)}, f32[1120]{0:T(1024)}) all-reduce(f32[1120]{0:T(1024)S(1)} %get-tuple-element.16, ...), channel_id=1, replica_groups=mesh['dp'=8,'tensor'=4] {'dp'}, use_global_device_ids=true, to_apply=%region_16.17 | all-reduce | flops 8400 | bytes 67200 | tf_op jit(solution)/shard_map/psum | solution.py:147
  332.2 2.5 fusion.103
  339.0 463.3 %all-reduce.10.cloned.1.call-done = (f32[1120,3,280]{0,2,1:T(8,128)}, f32[280,1120]{1,0:T(8,128)}, f32[1120,1120]{1,0:T(8,128)}, f32[1120,1120]{1,0:T(8,128)}) async-done(((f32[1120,3,280]{0,2,1:T(8,128)}, f32[280,1120]{1,0:T(8,128)}, f32[1120,1120]{1,0:T(8,128)}, f32[1120,1120]{1,0:T(8,128)}), (f32[1120,3,280]{0,2,1:T(8,128)}, f32[280,1120]{1,0:T(8,128)}, f32[1120,1120]{1,0:T(8,128)}, ...) | async-done | bytes 15052816 | tf_op jit(solution)/shard_map/psum | solution.py:147
  802.4 4.5 copy.98
  807.9 2.6 copy.100
  (127 shorter events, 38.0 us)
Async XLA Ops:
  7.2 132.3 %copy-start = (bf16[1120,1120]{1,0:T(8,128)(2,1)S(1)}, bf16[1120,1120]{1,0:T(8,128)(2,1)}, u32[]{:S(2)}) copy-start(bf16[1120,1120]{1,0:T(8,128)(2,1)} %param.24) | copy-start | bytes 7526404
  7.2 29.5 %copy-start.24 = (f32[1120]{0:T(1024)S(1)}, f32[1120]{0:T(1024)}, u32[]{:S(2)}) copy-start(f32[1120]{0:T(1024)} %param.17) | copy-start | bytes 13444
  7.2 29.5 %copy-start.20 = (f32[1120]{0:T(1024)S(1)}, f32[1120]{0:T(1024)}, u32[]{:S(2)}) copy-start(f32[1120]{0:T(1024)} %param.16) | copy-start | bytes 13444
  7.2 25.6 %all-gather.5.cloned.1.call-start = ((), (), s32[]{:S(2)}) async-start(), calls=%async_computation.1 | async-start | bytes 2150400 | tf_op jit(solution)/shard_map/all_gather | solution.py:47
  8.0 53.7 %all-gather.7.cloned.1.call-start = ((), (), s32[]{:S(2)}) async-start(), calls=%async_computation.3 | async-start | bytes 2150400 | tf_op jit(solution)/shard_map/all_gather | solution.py:93
  8.7 102.8 %all-gather.9.cloned.1.call-start = ((), (), s32[]{:S(2)}) async-start(), calls=%async_computation.6 | async-start | bytes 8601600 | tf_op jit(solution)/shard_map/all_gather | solution.py:77
  32.8 3.9 copy-start.5
  54.6 3.4 copy-start.28
  54.6 4.6 copy-start.16
  61.6 137.7 %all-reduce.6.cloned.1.call-start = ((), (), s32[]{:S(2)}) async-start(), calls=%async_computation.4 | async-start | bytes 3440640 | tf_op jit(solution)/shard_map/psum | solution.py:106
  125.2 11.2 %copy-start.21 = (f32[1120]{0:T(1024)S(1)}, f32[1120]{0:T(1024)}, u32[]{:S(2)}) copy-start(f32[1120]{0:T(1024)} %param.21) | copy-start | bytes 13444
  139.0 9.9 %copy-start.2 = (f32[768,1120]{0,1:T(8,128)}, f32[768,1120]{0,1:T(8,128)S(1)}, u32[]{:S(2)}) copy-start(f32[768,1120]{0,1:T(8,128)S(1)} %get-tuple-element.42) | copy-start | bytes 10321924
  153.7 137.4 %all-reduce.8.cloned.1.call-start = ((), (), s32[]{:S(2)}) async-start(), calls=%async_computation.5 | async-start | bytes 3440640 | tf_op jit(solution)/shard_map/psum | solution.py:142
  199.2 3.7 copy-start.9
  202.9 3.9 copy-start.3
  202.9 3.9 copy-start.12
  206.8 3.8 copy-start.17
  215.4 3.7 copy-start.15
  219.1 9.7 %copy-start.18 = (bf16[2,384,5,56]{1,0,3,2:T(2,128)(2,1)S(1)}, bf16[2,384,5,56]{1,0,3,2:T(2,128)(2,1)}, u32[]{:S(2)}) copy-start(bf16[2,384,5,56]{1,0,3,2:T(2,128)(2,1)} %convert_element_type.95) | copy-start | bytes 1290244
  245.5 91.3 %reduce-scatter.2.cloned.1.call-start = ((), (), s32[]{:S(2)}) async-start(), calls=%async_computation.2 | async-start | bytes 2150400 | tf_op jit(solution)/shard_map/reduce_scatter | solution.py:87
  245.6 6.8 copy-start.13
  252.4 550.0 %all-reduce.10.cloned.1.call-start = ((), (), s32[]{:S(2)}) async-start(), calls=%async_computation.7 | async-start | bytes 30965760 | tf_op jit(solution)/shard_map/psum | solution.py:147
  252.4 7.5 copy-start.4
  252.4 7.5 copy-start.27
  260.0 5.1 copy-start.8
  260.0 5.1 copy-start.11
  802.4 5.5 slice-start.2
  802.4 4.5 copy-start.14
  802.4 5.5 slice-start.3
  806.8 4.3 slice-start
  807.9 3.9 slice-start.1
  807.9 6.2 copy-start.1
  (9 other events, 13.8 us)
Sparse Core Ops, SparseCore 0:
  9.6 23.1 all-gather.4
  34.4 20.4 all-gather.6
  61.7 49.7 all-gather.8
  153.8 45.4 all-reduce.5
  245.6 45.4 all-reduce.7
  293.5 28.8 reduce-scatter.1
  328.3 473.9 all-reduce.9
